TPU v7x, 128 devices: a whole 4x4x4 slice. The times are simulated.
128 devices in a mesh: tile: 16 (over z, x_hi, core), win: 8 (over y, x_lo).
Axes of the slice: x: 4 (x_hi: 2, x_lo: 2; x = x_hi * 2 + x_lo), y: 4, z: 4, core: 2. Of those that a mesh axis runs over, the one named last changes fastest.
Arguments:
- initial_state: float32 [8, 4, 8, 64, 2048], P('win', None, None, None, 'tile'), may hold values from -6 to 6
- observed: float32 [8, 4, 8, 64, 2048], P('win', None, None, None, 'tile'), may hold values from -6 to 6
- mixing: float32 [8, 64, 2048], P(None, None, 'tile'), may hold values from 0.02 to 0.2
- velocity: float32 [8, 64, 2048], P(None, None, 'tile'), may hold values from 0 to 0.15
- sea_mask: int32 [8, 64, 2048], P(None, None, 'tile'), may hold values 0 or 1
- partner: int32 [2048], P('tile'), may hold values from 0 to 2047, as said below
Outputs:
- state_gradient: float32 [8, 4, 8, 64, 2048], P('win', None, None, None, 'tile')
- mixing_gradient: float32 [8, 64, 2048], P(None, 'win', 'tile')
Inputs may be any that keep to these rules, and one draw needn't show every extreme that they name: partner[i] = (s - i) mod 2048 for one whole number s of each draw, so that partner is its own inverse.
All inputs are finite; a program needn't handle non-finite values. No bound on the sum of `sea_mask` on one device may be relied on, other than what follows from the above.
Results may differ from a plain program's by a relative error of at most 0.00002.
Values sent between devices are 32-bit elements; how exact they have to be, the bound alone decides.
No kernel may reach another device: no remote copies, remote signals or barrier semaphores. Data moves between devices by JAX's collectives and lax.ppermute only.
A program may use at most 128 MiB of HBM per device.

v0:
```python
import jax
import jax.numpy as jnp
from jax import lax
from jax.sharding import PartitionSpec as P

STEPS = 6


def padded_2(cells, sides, width):
    for axis, dim in sides:
        count = lax.axis_size(axis)
        head = lax.slice_in_dim(cells, 0, width, axis=dim)
        tail = lax.slice_in_dim(cells, cells.shape[dim] - width, cells.shape[dim], axis=dim)
        cells = jnp.concatenate(
            [
                lax.ppermute(tail, axis, [(i, (i + 1) % count) for i in range(count)]),
                cells,
                lax.ppermute(head, axis, [((i + 1) % count, i) for i in range(count)]),
            ],
            axis=dim,
        )
    return cells


def passed_along(block, axis, distance):
    devices = range(lax.axis_size(axis))
    route = [(i - distance, i) for i in devices if i - distance in devices]
    return lax.ppermute(block, axis, route)


def passed_along_2(value, axis, steps):
    count = lax.axis_size(axis)
    pairs = [(source, (source + steps) % count) for source in range(count)]
    return lax.ppermute(value, axis, pairs)


def north_south(field, ghost_row):
    north = jnp.concatenate([field[..., 1:, :], ghost_row[..., None, :]], axis=-2)
    south = jnp.concatenate([jnp.zeros_like(field[..., :1, :]), field[..., :-1, :]], axis=-2)
    return (north, south)


def advance(
    centre,
    east,
    west,
    north,
    south,
    mixing,
    velocity,
    wet,
    wet_east,
    wet_west,
    wet_north,
    wet_south,
):
    spread = (
        wet_east * (east - centre)
        + wet_west * (west - centre)
        + wet_north * (north - centre)
        + wet_south * (south - centre)
    )
    return centre + wet * (mixing * spread - velocity * wet_west * (centre - west))


def with_columns(field):
    return padded_2(field, (("tile", 3),), 1)


def fold_ghost(top_rows, partner):
    gathered = lax.all_gather(top_rows, "tile", axis=2, tiled=True)
    return jnp.take(gathered, partner, axis=2)


def body(initial_state, observed, mixing, velocity, sea_mask, partner):
    start = initial_state[0]
    target = observed[0]
    wet = sea_mask.astype(jnp.float32)
    wet_padded = with_columns(wet[None])[0]
    wet_east = wet_padded[..., 2:]
    wet_west = wet_padded[..., :-2]
    wet_fold = fold_ghost(wet[None][:, :, -1, :], partner)[0]
    wet_north, wet_south = north_south(wet, wet_fold)
    window = lax.axis_index("win")

    def local_step(padded, ghost_row, coeff):
        centre = padded[..., 1:-1]
        north, south = north_south(centre, ghost_row)
        return advance(
            centre,
            padded[..., 2:],
            padded[..., :-2],
            north,
            south,
            coeff,
            velocity,
            wet,
            wet_east,
            wet_west,
            wet_north,
            wet_south,
        )

    field = start
    stored = []
    for moment in range(STEPS):
        padded = with_columns(field)
        ghost_row = fold_ghost(field[:, :, -1, :], partner)
        stored.append((padded, ghost_row))
        field = local_step(padded, ghost_row, mixing)
    previous_end = passed_along(field, "win", 1)
    mismatch = jnp.where(window > 0, start - previous_end, jnp.zeros_like(start))
    next_mismatch = passed_along(mismatch, "win", -1)
    adjoint = wet * (field - target) - next_mismatch
    mixing_sum = jnp.zeros_like(mixing)
    for moment in range(STEPS - 1, -1, -1):
        padded, ghost_row = stored[moment]
        _, pullback = jax.vjp(local_step, padded, ghost_row, mixing)
        padded_part, ghost_part, mixing_part = pullback(adjoint)
        mixing_sum = mixing_sum + mixing_part
        from_right = passed_along_2(padded_part[..., 0], "tile", -1)
        from_left = passed_along_2(padded_part[..., -1], "tile", 1)
        adjoint = padded_part[..., 1:-1]
        adjoint = adjoint.at[..., -1].add(from_right)
        adjoint = adjoint.at[..., 0].add(from_left)
        adjoint = adjoint.at[:, :, -1, :].add(fold_ghost(ghost_part, partner))
    state_gradient = adjoint + mismatch
    mixing_gradient = lax.psum_scatter(mixing_sum, "win", scatter_dimension=1, tiled=True)
    return (state_gradient[None], mixing_gradient)


def solution(mesh):
    in_specs = (
        P("win", None, None, None, "tile"),
        P("win", None, None, None, "tile"),
        P(None, None, "tile"),
        P(None, None, "tile"),
        P(None, None, "tile"),
        P("tile"),
    )
    out_specs = (P("win", None, None, None, "tile"), P(None, "win", "tile"))
    return jax.shard_map(body, mesh=mesh, in_specs=in_specs, out_specs=out_specs, check_vma=False)
```

profile of v0, /device:TPU:1, one launch (start us, length us, event | category | flops | bytes accessed | tf_op | source)
XLA Modules:
  0.0 869.9 jit_solution(5114606061097768946)
XLA Ops:
  9.5 4.2 collective-permute-start.3
  16.8 5.0 fusion.106
  21.9 3.3 collective-permute-start
  26.9 26.8 %all-gather.1 = f32[4,8,1,2048]{3,1,2,0:T(8,128)S(1)} all-gather(f32[4,8,1,128]{3,1,2,0:T(8,128)S(1)} %bitcast.138), channel_id=3, replica_groups=mesh['tile'=16,'win'=8] {'tile'}, dimensions={3}, use_global_device_ids=true | all-gather | bytes 278528 | tf_op jit(solution)/shard_map/all_gather | solution.py:71
  53.7 3.1 copy.1359
  56.8 26.0 %all-gather = f32[1,8,1,2048]{1,3,2,0:T(8,128)S(1)} all-gather(f32[1,8,1,128]{1,3,2,0:T(8,128)S(1)} %slice.847), channel_id=2, replica_groups=mesh['tile'=16,'win'=8] {'tile'}, dimensions={3}, use_global_device_ids=true | all-gather | bytes 69632 | tf_op jit(solution)/shard_map/all_gather | solution.py:71
  86.7 6.3 fusion.105
  111.3 4.2 fusion.65
  118.9 21.4 %all-gather.2 = f32[4,8,1,2048]{3,1,2,0:T(8,128)S(1)} all-gather(f32[4,8,1,128]{3,1,2,0:T(8,128)S(1)} %bitcast.139), channel_id=4, replica_groups=mesh['tile'=16,'win'=8] {'tile'}, dimensions={3}, use_global_device_ids=true | all-gather | bytes 278528 | tf_op jit(solution)/shard_map/all_gather | solution.py:71
  145.4 3.1 copy.1368
  154.5 5.2 fusion.53
  163.2 23.8 %all-gather.3 = f32[4,8,1,2048]{3,1,2,0:T(8,128)S(1)} all-gather(f32[4,8,1,128]{3,1,2,0:T(8,128)S(1)} %bitcast.140), channel_id=5, replica_groups=mesh['tile'=16,'win'=8] {'tile'}, dimensions={3}, use_global_device_ids=true | all-gather | bytes 278528 | tf_op jit(solution)/shard_map/all_gather | solution.py:71
  202.3 5.1 fusion.41
  210.9 23.6 %all-gather.4 = f32[4,8,1,2048]{3,1,2,0:T(8,128)S(1)} all-gather(f32[4,8,1,128]{3,1,2,0:T(8,128)S(1)} %bitcast.141), channel_id=6, replica_groups=mesh['tile'=16,'win'=8] {'tile'}, dimensions={3}, use_global_device_ids=true | all-gather | bytes 278528 | tf_op jit(solution)/shard_map/all_gather | solution.py:71
  248.8 5.1 fusion.29
  257.4 23.6 %all-gather.5 = f32[4,8,1,2048]{3,1,2,0:T(8,128)S(1)} all-gather(f32[4,8,1,128]{3,1,2,0:T(8,128)S(1)} %bitcast.142), channel_id=7, replica_groups=mesh['tile'=16,'win'=8] {'tile'}, dimensions={3}, use_global_device_ids=true | all-gather | bytes 278528 | tf_op jit(solution)/shard_map/all_gather | solution.py:71
  287.3 3.1 copy.1392
  296.5 5.1 fusion.17
  305.1 23.6 %all-gather.6 = f32[4,8,1,2048]{3,1,2,0:T(8,128)S(1)} all-gather(f32[4,8,1,128]{3,1,2,0:T(8,128)S(1)} %bitcast.143), channel_id=8, replica_groups=mesh['tile'=16,'win'=8] {'tile'}, dimensions={3}, use_global_device_ids=true | all-gather | bytes 278528 | tf_op jit(solution)/shard_map/all_gather | solution.py:71
  343.0 5.7 fusion.5
  348.7 3.3 collective-permute-start.14
  352.0 18.4 %collective-permute-done.14 = f32[4,8,64,128]{3,2,1,0:T(8,128)} collective-permute-done((f32[4,8,64,128]{3,2,1,0:T(8,128)}, f32[4,8,64,128]{3,2,1,0:T(8,128)}, u32[]{:S(2)}, u32[]{:S(2)}) %collective-permute-start.14) | collective-permute-done | bytes 1048608 | tf_op jit(solution)/shard_map/ppermute | solution.py:28
  373.1 22.0 %collective-permute-done.15 = f32[4,8,64,128]{3,2,1,0:T(8,128)S(1)} collective-permute-done((f32[4,8,64,128]{3,2,1,0:T(8,128)S(1)}, f32[4,8,64,128]{3,2,1,0:T(8,128)S(1)}, u32[]{:S(2)}, u32[]{:S(2)}) %collective-permute-start.15) | collective-permute-done | bytes 1048608 | tf_op jit(solution)/shard_map/ppermute | solution.py:28
  397.6 32.6 %all-gather.7 = f32[4,8,1,2048]{3,1,2,0:T(8,128)S(1)} all-gather(f32[4,8,1,128]{3,1,2,0:T(8,128)S(1)} %bitcast.144), channel_id=9, replica_groups=mesh['tile'=16,'win'=8] {'tile'}, dimensions={3}, use_global_device_ids=true | all-gather | bytes 278528 | tf_op jit(solution)/shard_map/all_gather | solution.py:71
  442.7 3.6 collective-permute-start.17
  451.7 4.6 scatter-add.60
  465.6 21.0 %all-gather.8 = f32[4,8,1,2048]{3,1,2,0:T(8,128)S(1)} all-gather(f32[4,8,1,128]{3,1,2,0:T(8,128)S(1)} %bitcast.134), channel_id=10, replica_groups=mesh['tile'=16,'win'=8] {'tile'}, dimensions={3}, use_global_device_ids=true | all-gather | bytes 278528 | tf_op jit(solution)/shard_map/all_gather | solution.py:71
  500.2 4.6 scatter-add.65
  515.2 23.7 %all-gather.9 = f32[4,8,1,2048]{3,1,2,0:T(8,128)S(1)} all-gather(f32[4,8,1,128]{3,1,2,0:T(8,128)S(1)} %bitcast.135), channel_id=11, replica_groups=mesh['tile'=16,'win'=8] {'tile'}, dimensions={3}, use_global_device_ids=true | all-gather | bytes 278528 | tf_op jit(solution)/shard_map/all_gather | solution.py:71
  553.7 5.2 scatter-add.70
  561.6 3.6 scatter-add.71
  574.3 23.6 %all-gather.10 = f32[4,8,1,2048]{3,1,2,0:T(8,128)S(1)} all-gather(f32[4,8,1,128]{3,1,2,0:T(8,128)S(1)} %bitcast.136), channel_id=12, replica_groups=mesh['tile'=16,'win'=8] {'tile'}, dimensions={3}, use_global_device_ids=true | all-gather | bytes 278528 | tf_op jit(solution)/shard_map/all_gather | solution.py:71
  611.9 5.2 scatter-add.75
  619.8 3.7 scatter-add.76
  632.6 23.6 %all-gather.11 = f32[4,8,1,2048]{3,1,2,0:T(8,128)S(1)} all-gather(f32[4,8,1,128]{3,1,2,0:T(8,128)S(1)} %bitcast.137), channel_id=13, replica_groups=mesh['tile'=16,'win'=8] {'tile'}, dimensions={3}, use_global_device_ids=true | all-gather | bytes 278528 | tf_op jit(solution)/shard_map/all_gather | solution.py:71
  671.4 5.2 scatter-add.80
  679.3 3.6 scatter-add.81
  685.5 7.2 multiply_reduce_fusion.4
  696.6 23.6 %all-gather.12 = f32[4,8,1,2048]{3,1,2,0:T(8,128)S(1)} all-gather(f32[4,8,1,128]{3,1,2,0:T(8,128)S(1)} %bitcast.133), channel_id=14, replica_groups=mesh['tile'=16,'win'=8] {'tile'}, dimensions={3}, use_global_device_ids=true | all-gather | bytes 278528 | tf_op jit(solution)/shard_map/all_gather | solution.py:71
  728.3 4.4 copy.1468
  732.7 4.5 copy.1467
  737.2 4.4 copy.1469
  741.6 4.4 copy.1470
  746.0 4.4 copy.1471
  750.4 4.5 copy.1472
  754.9 13.9 %add_add_fusion = f32[8,64,128]{0,1,2:T(8,128)} fusion(f32[8,64,128]{0,1,2:T(8,128)} %copy.1472, f32[8,64,128]{0,1,2:T(8,128)} %copy.1471, f32[8,64,128]{0,1,2:T(8,128)} %copy.1470, f32[8,64,128]{0,1,2:T(8,128)} %copy.1469, f32[8,64,128]{0,1,2:T(8,128)} %copy.1467, f32[8,64,128]{0,1,2:T(8,128)} %copy.1468), kind=kLoop, calls=%fused_computation.14 | loop fusion | flops 327680 | bytes 1835008 | tf_op jit(solution)/shard_map/add | solution.py:120
  773.6 3.7 scatter-add.85
  782.4 78.7 %reduce-scatter.2.cloned.1.call-done = f32[8,8,128]{0,1,2:T(8,128)} async-done(((f32[8,64,128]{0,1,2:T(8,128)}), f32[8,8,128]{0,1,2:T(8,128)}) %reduce-scatter.2.cloned.1.call-update) | async-done | bytes 32784 | tf_op jit(solution)/shard_map/reduce_scatter | solution.py:128
  (295 shorter events, 266.2 us)
Async XLA Ops:
  7.2 7.0 copy-start.24
  7.2 853.9 %reduce-scatter.2.cloned.1.call-start = ((), (), s32[]{:S(2)}) async-start(), calls=%async_computation.1 | async-start | bytes 4718592 | tf_op jit(solution)/shard_map/reduce_scatter | solution.py:128
  9.5 100.4 %collective-permute-start.3 = (f32[4,8,64,1]{2,1,3,0:T(8,128)S(1)}, f32[4,8,64,1]{2,1,3,0:T(8,128)S(1)}, u32[]{:S(2)}, u32[]{:S(2)}) collective-permute-start(f32[4,8,64,1]{2,1,3,0:T(8,128)S(1)} %copy.1355), channel_id=1, source_target_pairs={{0,8},{8,16},{16,24},{24,32},{32,40},{40,48},{48,56},{56,64},{64,7... | collective-permute-start | bytes 24584 | tf_op jit(solution)/shard_map/ppermute | solution.py:16
  14.1 94.4 %collective-permute-start.2 = (f32[4,8,64,1]{2,1,3,0:T(8,128)S(1)}, f32[4,8,64,1]{2,1,3,0:T(8,128)S(1)}, u32[]{:S(2)}, u32[]{:S(2)}) collective-permute-start(f32[4,8,64,1]{2,1,3,0:T(8,128)S(1)} %copy.1353), channel_id=1, source_target_pairs={{8,0},{16,8},{24,16},{32,24},{40,32},{48,40},{56,48},{64,56},{72,6... | collective-permute-start | bytes 24584 | tf_op jit(solution)/shard_map/ppermute | solution.py:18
  16.8 8.5 copy-start.26
  16.8 8.5 copy-start.1
  21.8 5.0 copy-start.16
  21.9 85.7 %collective-permute-start = (f32[1,8,64,1]{1,3,2,0:T(1,128)S(1)}, f32[1,8,64,1]{1,3,2,0:T(1,128)S(1)}, u32[]{:S(2)}, u32[]{:S(2)}) collective-permute-start(f32[1,8,64,1]{1,3,2,0:T(1,128)S(1)} %get-tuple-element.279), channel_id=1, source_target_pairs={{0,8},{8,16},{16,24},{24,32},{32,40},{40,48},{48,56},{56,64},{64,7... | collective-permute-start | bytes 6152 | tf_op jit(solution)/shard_map/ppermute | solution.py:16
  25.1 82.0 %collective-permute-start.1 = (f32[1,8,64,1]{1,3,2,0:T(1,128)S(1)}, f32[1,8,64,1]{1,3,2,0:T(1,128)S(1)}, u32[]{:S(2)}, u32[]{:S(2)}) collective-permute-start(f32[1,8,64,1]{1,3,2,0:T(1,128)S(1)} %get-tuple-element.280), channel_id=1, source_target_pairs={{8,0},{16,8},{24,16},{32,24},{40,32},{48,40},{56,48},{64,56},{72,6... | collective-permute-start | bytes 6152 | tf_op jit(solution)/shard_map/ppermute | solution.py:18
  104.2 4.1 copy-start.25
  104.2 7.1 copy-start
  115.4 3.4 copy-start.6
  143.4 9.7 %collective-permute-start.5 = (f32[4,8,64,1]{2,1,3,0:T(8,128)S(1)}, f32[4,8,64,1]{2,1,3,0:T(8,128)S(1)}, u32[]{:S(2)}, u32[]{:S(2)}) collective-permute-start(f32[4,8,64,1]{2,1,3,0:T(8,128)S(1)} %copy.1365), channel_id=1, source_target_pairs={{0,8},{8,16},{16,24},{24,32},{32,40},{40,48},{48,56},{56,64},{64,7... | collective-permute-start | bytes 24584 | tf_op jit(solution)/shard_map/ppermute | solution.py:16
  145.2 6.5 collective-permute-start.4
  159.8 3.4 copy-start.2
  190.2 10.7 %collective-permute-start.7 = (f32[4,8,64,1]{2,1,3,0:T(8,128)S(1)}, f32[4,8,64,1]{2,1,3,0:T(8,128)S(1)}, u32[]{:S(2)}, u32[]{:S(2)}) collective-permute-start(f32[4,8,64,1]{2,1,3,0:T(8,128)S(1)} %copy.1373), channel_id=1, source_target_pairs={{0,8},{8,16},{16,24},{24,32},{32,40},{40,48},{48,56},{56,64},{64,7... | collective-permute-start | bytes 24584 | tf_op jit(solution)/shard_map/ppermute | solution.py:16
  193.2 6.3 collective-permute-start.6
  207.4 3.4 copy-start.3
  237.7 9.7 %collective-permute-start.9 = (f32[4,8,64,1]{2,1,3,0:T(8,128)S(1)}, f32[4,8,64,1]{2,1,3,0:T(8,128)S(1)}, u32[]{:S(2)}, u32[]{:S(2)}) collective-permute-start(f32[4,8,64,1]{2,1,3,0:T(8,128)S(1)} %copy.1381), channel_id=1, source_target_pairs={{0,8},{8,16},{16,24},{24,32},{32,40},{40,48},{48,56},{56,64},{64,7... | collective-permute-start | bytes 24584 | tf_op jit(solution)/shard_map/ppermute | solution.py:16
  239.7 6.3 collective-permute-start.8
  253.9 3.4 copy-start.4
  284.2 10.9 %collective-permute-start.11 = (f32[4,8,64,1]{2,1,3,0:T(8,128)S(1)}, f32[4,8,64,1]{2,1,3,0:T(8,128)S(1)}, u32[]{:S(2)}, u32[]{:S(2)}) collective-permute-start(f32[4,8,64,1]{2,1,3,0:T(8,128)S(1)} %copy.1389), channel_id=1, source_target_pairs={{0,8},{8,16},{16,24},{24,32},{32,40},{40,48},{48,56},{56,64},{64,7... | collective-permute-start | bytes 24584 | tf_op jit(solution)/shard_map/ppermute | solution.py:16
  287.1 6.5 collective-permute-start.10
  301.6 3.4 copy-start.5
  331.8 9.7 %collective-permute-start.13 = (f32[4,8,64,1]{2,1,3,0:T(8,128)S(1)}, f32[4,8,64,1]{2,1,3,0:T(8,128)S(1)}, u32[]{:S(2)}, u32[]{:S(2)}) collective-permute-start(f32[4,8,64,1]{2,1,3,0:T(8,128)S(1)} %copy.1397), channel_id=1, source_target_pairs={{0,8},{8,16},{16,24},{24,32},{32,40},{40,48},{48,56},{56,64},{64,7... | collective-permute-start | bytes 24584 | tf_op jit(solution)/shard_map/ppermute | solution.py:16
  333.8 6.3 collective-permute-start.12
  348.7 21.7 %collective-permute-start.14 = (f32[4,8,64,128]{3,2,1,0:T(8,128)}, f32[4,8,64,128]{3,2,1,0:T(8,128)}, u32[]{:S(2)}, u32[]{:S(2)}) collective-permute-start(f32[4,8,64,128]{3,2,1,0:T(8,128)} %get-tuple-element.263), channel_id=1, source_target_pairs={{0,1},{1,2},{2,3},{3,4},{4,5},{5,6},{6,7},{8,9},{9,10},{10,11},{11... | collective-permute-start | bytes 3145736 | tf_op jit(solution)/shard_map/ppermute | solution.py:28
  371.8 23.3 %collective-permute-start.15 = (f32[4,8,64,128]{3,2,1,0:T(8,128)S(1)}, f32[4,8,64,128]{3,2,1,0:T(8,128)S(1)}, u32[]{:S(2)}, u32[]{:S(2)}) collective-permute-start(f32[4,8,64,128]{3,2,1,0:T(8,128)S(1)} %subtract_select_fusion), channel_id=1, source_target_pairs={{1,0},{2,1},{3,2},{4,3},{5,4},{6,5},{7,6},{9,8},{10,9},{11,10},{12... | collective-permute-start | bytes 3145736 | tf_op jit(solution)/shard_map/ppermute | solution.py:28
  397.1 33.8 %copy-start.18 = (f32[4,8,64,128]{3,2,1,0:T(8,128)}, f32[4,8,64,128]{3,2,1,0:T(8,128)S(1)}, u32[]{:S(2)}) copy-start(f32[4,8,64,128]{3,2,1,0:T(8,128)S(1)} %get-tuple-element.262) | copy-start | bytes 3145732
  434.4 11.8 %collective-permute-start.16 = (f32[4,8,64]{2,1,0:T(8,128)S(1)}, f32[4,8,64]{2,1,0:T(8,128)S(1)}, u32[]{:S(2)}, u32[]{:S(2)}) collective-permute-start(f32[4,8,64]{2,1,0:T(8,128)S(1)} %get-tuple-element.254), channel_id=1, source_target_pairs={{0,120},{8,0},{16,8},{24,16},{32,24},{40,32},{48,40},{56,48},{64,5... | collective-permute-start | bytes 24584 | tf_op jit(solution)/shard_map/ppermute | solution.py:34
  442.7 7.6 collective-permute-start.17
  486.6 12.2 %collective-permute-start.19 = (f32[4,8,64]{2,1,0:T(8,128)S(1)}, f32[4,8,64]{2,1,0:T(8,128)S(1)}, u32[]{:S(2)}, u32[]{:S(2)}) collective-permute-start(f32[4,8,64]{2,1,0:T(8,128)S(1)} %get-tuple-element.251), channel_id=1, source_target_pairs={{0,8},{8,16},{16,24},{24,32},{32,40},{40,48},{48,56},{56,64},{64,7... | collective-permute-start | bytes 24584 | tf_op jit(solution)/shard_map/ppermute | solution.py:34
  488.3 6.3 collective-permute-start.18
  538.9 13.4 %collective-permute-start.21 = (f32[4,8,64]{2,1,0:T(8,128)S(1)}, f32[4,8,64]{2,1,0:T(8,128)S(1)}, u32[]{:S(2)}, u32[]{:S(2)}) collective-permute-start(f32[4,8,64]{2,1,0:T(8,128)S(1)} %get-tuple-element.249), channel_id=1, source_target_pairs={{0,8},{8,16},{16,24},{24,32},{32,40},{40,48},{48,56},{56,64},{64,7... | collective-permute-start | bytes 24584 | tf_op jit(solution)/shard_map/ppermute | solution.py:34
  541.8 6.3 collective-permute-start.20
  567.7 1.7 copy-start.7
  597.9 12.6 %collective-permute-start.23 = (f32[4,8,64]{2,1,0:T(8,128)S(1)}, f32[4,8,64]{2,1,0:T(8,128)S(1)}, u32[]{:S(2)}, u32[]{:S(2)}) collective-permute-start(f32[4,8,64]{2,1,0:T(8,128)S(1)} %get-tuple-element.247), channel_id=1, source_target_pairs={{0,8},{8,16},{16,24},{24,32},{32,40},{40,48},{48,56},{56,64},{64,7... | collective-permute-start | bytes 24584 | tf_op jit(solution)/shard_map/ppermute | solution.py:34
  599.8 6.5 collective-permute-start.22
  626.1 1.7 copy-start.8
  656.2 13.8 %collective-permute-start.25 = (f32[4,8,64]{2,1,0:T(8,128)S(1)}, f32[4,8,64]{2,1,0:T(8,128)S(1)}, u32[]{:S(2)}, u32[]{:S(2)}) collective-permute-start(f32[4,8,64]{2,1,0:T(8,128)S(1)} %get-tuple-element.245), channel_id=1, source_target_pairs={{0,8},{8,16},{16,24},{24,32},{32,40},{40,48},{48,56},{56,64},{64,7... | collective-permute-start | bytes 24584 | tf_op jit(solution)/shard_map/ppermute | solution.py:34
  659.1 6.7 collective-permute-start.24
  685.5 7.4 copy-start.17
  694.9 33.4 %copy-start.23 = (f32[8,64,128]{2,1,0:T(8,128)S(1)}, f32[8,64,128]{2,1,0:T(8,128)}, u32[]{:S(2)}) copy-start(f32[8,64,128]{2,1,0:T(8,128)} %get-tuple-element.255) | copy-start | bytes 786436
  720.2 52.0 %collective-permute-start.27 = (f32[4,8,64]{2,1,0:T(8,128)S(1)}, f32[4,8,64]{2,1,0:T(8,128)S(1)}, u32[]{:S(2)}, u32[]{:S(2)}) collective-permute-start(f32[4,8,64]{2,1,0:T(8,128)S(1)} %get-tuple-element.243), channel_id=1, source_target_pairs={{0,8},{8,16},{16,24},{24,32},{32,40},{40,48},{48,56},{56,64},{64,7... | collective-permute-start | bytes 24584 | tf_op jit(solution)/shard_map/ppermute | solution.py:34
  722.1 47.0 %collective-permute-start.26 = (f32[4,8,64]{2,1,0:T(8,128)S(1)}, f32[4,8,64]{2,1,0:T(8,128)S(1)}, u32[]{:S(2)}, u32[]{:S(2)}) collective-permute-start(f32[4,8,64]{2,1,0:T(8,128)S(1)} %get-tuple-element.244), channel_id=1, source_target_pairs={{0,120},{8,0},{16,8},{24,16},{32,24},{40,32},{48,40},{56,48},{64,5... | collective-permute-start | bytes 24584 | tf_op jit(solution)/shard_map/ppermute | solution.py:34
  722.3 10.5 %copy-start.22 = (f32[8,64,128]{2,1,0:T(8,128)S(1)}, f32[8,64,128]{2,1,0:T(8,128)}, u32[]{:S(2)}) copy-start(f32[8,64,128]{2,1,0:T(8,128)} %get-tuple-element.256) | copy-start | bytes 786436
  728.3 8.9 %copy-start.21 = (f32[8,64,128]{2,1,0:T(8,128)S(1)}, f32[8,64,128]{2,1,0:T(8,128)}, u32[]{:S(2)}) copy-start(f32[8,64,128]{2,1,0:T(8,128)} %get-tuple-element.257) | copy-start | bytes 786436
  732.7 8.9 %copy-start.20 = (f32[8,64,128]{2,1,0:T(8,128)S(1)}, f32[8,64,128]{2,1,0:T(8,128)}, u32[]{:S(2)}) copy-start(f32[8,64,128]{2,1,0:T(8,128)} %get-tuple-element.258) | copy-start | bytes 786436
  (8 other events, 10.8 us)
Sparse Core Ops, SparseCore 0:
  769.2 91.7 reduce-scatter.1
where the time goes:
time: 880 us; the launch traced here: 870 us
  blocking collectives  317 us (36%)
  local copies, waits for them, and re-layouts  262 us (30%)
  waiting for transfers between devices  119 us (14%)
  other arithmetic  116 us (13%)
  starting transfers between devices  40.3 us (5%)
  between operations  15.2 us (2%)
    all_gather x13, blocking collectives, fold_ghost(): gathered = lax.all_gather(top_rows, 'tile', axis=2, tiled=True)  317 us
    reduce_scatter x1, waiting for transfers between devices, body(): lax.psum_scatter(mixing_sum, 'win', scatter_dimension=1, tiled=True)  78.7 us
    ppermute x2, waiting for transfers between devices, passed_along(): return lax.ppermute(block, axis, route)  40.4 us
    unnamed x63, local copies, waits for them, and re-layouts  37.6 us
    all_gather x12, local copies, waits for them, and re-layouts, fold_ghost(): gathered = lax.all_gather(top_rows, 'tile', axis=2, tiled=True)  36.9 us
    gather x14, local copies, waits for them, and re-layouts, fold_ghost(): return jnp.take(gathered, partner, axis=2)  36.1 us
    add x6, other arithmetic, advance(): centre + wet * (mixing * spread - velocity * wet_west * (centre - west))  30.6 us
    scatter-add x6, local copies, waits for them, and re-layouts, body(): adjoint = adjoint.at[..., -1].add(from_right)  28.5 us
  transfers between devices with their start and end apart: 29, of which 3 were waited for; matrix products, arithmetic and copies ran while one was open for 22% of the time, Pallas kernels for 0%

commit v1 on v0

--- a/solution.py
+++ b/solution.py
@@ -68,7 +68,9 @@
 
 
 def fold_ghost(top_rows, partner):
-    gathered = lax.all_gather(top_rows, "tile", axis=2, tiled=True)
+    gathered = jnp.concatenate(
+        lax.all_to_all(jnp.stack([top_rows] * lax.axis_size("tile")), "tile", 0, 0), axis=2
+    )
     return jnp.take(gathered, partner, axis=2)
 
 

time: 880 us -> 733 us (0.83)
  blocking collectives: 317 us -> 0 us
  local copies, waits for them, and re-layouts: 262 us -> 392 us
  starting transfers between devices: 40.3 us -> 144 us
  waiting for transfers between devices: 119 us -> 71 us
  other arithmetic: 116 us -> 95.2 us
    all_gather x13 -> x0, blocking collectives: 317 us -> none  [fold_ghost(): gathered = lax.all_gather(top_rows, 'tile', axis=2, tiled=True)]
    scatter-add x6, local copies, waits for them, and re-layouts: 28.5 us -> 130 us  [body(): adjoint = adjoint.at[..., -1].add(from_right)]
    all_to_all x0 -> x13, starting transfers between devices: none -> 98 us  [fold_ghost(): lax.all_to_all(jnp.stack([top_rows] * lax.axis_size('tile')), 'tile', 0, 0)]
    reduce_scatter x1, waiting for transfers between devices: 78.7 us -> 0.01 us  [body(): lax.psum_scatter(mixing_sum, 'win', scatter_dimension=1, tiled=True)]
    reshape x0 -> x13, local copies, waits for them, and re-layouts: none -> 38 us  [fold_ghost(): jnp.concatenate(lax.all_to_all(jnp.stack([top_rows] * lax.axis_size('tile...]
    all_gather x12 -> x0, local copies, waits for them, and re-layouts: 36.9 us -> none  [fold_ghost(): gathered = lax.all_gather(top_rows, 'tile', axis=2, tiled=True)]
    unnamed x63 -> x75, local copies, waits for them, and re-layouts: 37.6 us -> 13.4 us
    another operation x17 -> x37, local copies, waits for them, and re-layouts: 17.3 us -> 35 us
  transfers between devices with their start and end apart: 29 -> 42, of which waited for: 3 -> 9; matrix products, arithmetic and copies ran while one was open for 22% -> 42% of each run, Pallas kernels for 0% -> 0%
where the time goes in v1:
time: 733 us; the launch traced here: 718 us
  local copies, waits for them, and re-layouts  392 us (53%)
  starting transfers between devices  144 us (20%)
  other arithmetic  95.2 us (13%)
  waiting for transfers between devices  71 us (10%)
  between operations  15.6 us (2%)
    scatter-add x6, local copies, waits for them, and re-layouts, body(): adjoint = adjoint.at[..., -1].add(from_right)  130 us
    all_to_all x13, starting transfers between devices, fold_ghost(): lax.all_to_all(jnp.stack([top_rows] * lax.axis_size('tile')), 'tile', 0, 0)  98 us
    ppermute x2, waiting for transfers between devices, passed_along(): return lax.ppermute(block, axis, route)  49.1 us
    reshape x13, local copies, waits for them, and re-layouts, fold_ghost(): jnp.concatenate(lax.all_to_all(jnp.stack([top_rows] * lax.axis_size('tile...  38 us
    gather x13, local copies, waits for them, and re-layouts, fold_ghost(): return jnp.take(gathered, partner, axis=2)  37.3 us
    scatter-add x6, local copies, waits for them, and re-layouts, body(): adjoint = adjoint.at[..., 0].add(from_left)  26.4 us
    add x6, other arithmetic, advance(): centre + wet * (mixing * spread - velocity * wet_west * (centre - west))  25.7 us
    ppermute x7, starting transfers between devices, padded_2(): lax.ppermute(tail, axis, [(i, (i + 1) % count) for i in range(count)])  22.2 us
  transfers between devices with their start and end apart: 42, of which 9 were waited for; matrix products, arithmetic and copies ran while one was open for 42% of the time, Pallas kernels for 0%

profile of v1, /device:TPU:1, one launch (start us, length us, event | category | flops | bytes accessed | tf_op | source)
XLA Modules:
  0.0 718.5 jit_solution(13161174651971371311)
XLA Ops:
  8.8 9.3 %all-to-all-start = ((f32[16,1,8,128]{3,2,1,0:T(8,128)}), f32[16,1,8,128]{3,2,1,0:T(8,128)S(1)}, u32[]{:S(2)}, u32[]{:S(2)}) async-start(f32[16,1,8,128]{3,2,1,0:T(8,128)} %stack.38), calls=%async_computation | async-start | bytes 131072 | tf_op jit(solution)/shard_map/all_to_all | solution.py:72
  19.0 3.1 collective-permute-start
  27.4 3.3 collective-permute-start.3
  42.4 7.8 %all-to-all-start.1 = ((f32[16,4,8,128]{3,2,1,0:T(8,128)}), f32[16,4,8,128]{3,2,1,0:T(8,128)S(1)}, u32[]{:S(2)}, u32[]{:S(2)}) async-start(f32[16,4,8,128]{3,2,1,0:T(8,128)} %stack.39), calls=%async_computation.1 | async-start | bytes 524288 | tf_op jit(solution)/shard_map/all_to_all | solution.py:72
  53.8 5.1 all-to-all-done.1
  65.2 4.2 fusion.65
  71.8 4.4 all-to-all-start.2
  79.8 3.2 collective-permute-start.5
  97.8 4.2 fusion.53
  104.4 6.1 all-to-all-start.3
  114.0 3.2 collective-permute-start.7
  131.8 4.3 fusion.41
  138.5 6.0 all-to-all-start.4
  148.1 3.2 collective-permute-start.9
  166.2 4.2 fusion.29
  172.8 6.0 all-to-all-start.5
  182.4 3.2 collective-permute-start.11
  200.2 4.2 fusion.17
  206.8 6.0 all-to-all-start.6
  216.3 3.2 collective-permute-start.13
  221.2 3.1 collective-permute-done.12
  234.2 4.6 fusion.5
  241.1 22.9 %collective-permute-done.14 = f32[4,8,64,128]{3,1,0,2:T(8,128)S(1)} collective-permute-done((f32[4,8,64,128]{3,1,0,2:T(8,128)}, f32[4,8,64,128]{3,1,0,2:T(8,128)S(1)}, u32[]{:S(2)}, u32[]{:S(2)}) %collective-permute-start.14) | collective-permute-done | bytes 1048608 | tf_op jit(solution)/shard_map/ppermute | solution.py:28
  267.3 26.2 %collective-permute-done.15 = f32[4,8,64,128]{3,1,0,2:T(8,128)S(1)} collective-permute-done((f32[4,8,64,128]{3,1,0,2:T(8,128)S(1)}, f32[4,8,64,128]{3,1,0,2:T(8,128)S(1)}, u32[]{:S(2)}, u32[]{:S(2)}) %collective-permute-start.15) | collective-permute-done | bytes 1048608 | tf_op jit(solution)/shard_map/ppermute | solution.py:28
  309.8 7.1 all-to-all-start.7
  323.3 21.5 %scatter-add.60 = f32[4,8,64,128]{3,1,0,2:T(8,128)S(1)} dynamic-update-slice(f32[4,8,64,128]{3,1,0,2:T(8,128)S(1)} %slice.877, f32[4,8,64,1]{3,1,0,2:T(8,128)} %slice_add_fusion.11, s32[]{:T(128)} %constant.410.clone.1, s32[]{:T(128)} %constant.410.clone.1, s32[]{:T(128)} %constant.410.clone.1, s32[]{:T(128)} %constant.416.clone.1) | dynamic-update-slice | bytes 16388 | tf_op jit(solution)/shard_map/scatter-add | solution.py:126
  347.2 4.0 scatter-add.61
  366.5 3.2 collective-permute-start.19
  374.1 9.3 %all-to-all-start.8 = ((f32[16,4,8,128]{3,2,1,0:T(8,128)}), f32[16,4,8,128]{3,2,1,0:T(8,128)S(1)}, u32[]{:S(2)}, u32[]{:S(2)}) async-start(f32[16,4,8,128]{3,2,1,0:T(8,128)} %stack.48), calls=%async_computation.8 | async-start | bytes 524288 | tf_op jit(solution)/shard_map/all_to_all | solution.py:72
  389.8 22.0 %scatter-add.65 = f32[4,8,64,128]{3,1,0,2:T(8,128)} dynamic-update-slice(f32[4,8,64,128]{3,1,0,2:T(8,128)} %slice.883, f32[4,8,64,1]{3,1,0,2:T(8,128)} %slice_add_fusion.9, s32[]{:T(128)} %constant.410.clone.1, s32[]{:T(128)} %constant.410.clone.1, s32[]{:T(128)} %constant.410.clone.1, s32[]{:T(128)} %constant.416.clone.1) | dynamic-update-slice | bytes 16388 | tf_op jit(solution)/shard_map/scatter-add | solution.py:126
  414.5 4.7 scatter-add.66
  437.5 3.2 collective-permute-start.21
  445.1 9.0 %all-to-all-start.9 = ((f32[16,4,8,128]{3,2,1,0:T(8,128)}), f32[16,4,8,128]{3,2,1,0:T(8,128)S(1)}, u32[]{:S(2)}, u32[]{:S(2)}) async-start(f32[16,4,8,128]{3,2,1,0:T(8,128)} %stack.50), calls=%async_computation.9 | async-start | bytes 524288 | tf_op jit(solution)/shard_map/all_to_all | solution.py:72
  460.6 22.0 %scatter-add.70 = f32[4,8,64,128]{3,1,0,2:T(8,128)} dynamic-update-slice(f32[4,8,64,128]{3,1,0,2:T(8,128)} %slice.889, f32[4,8,64,1]{3,1,0,2:T(8,128)} %slice_add_fusion.7, s32[]{:T(128)} %constant.410.clone.1, s32[]{:T(128)} %constant.410.clone.1, s32[]{:T(128)} %constant.410.clone.1, s32[]{:T(128)} %constant.416.clone.1) | dynamic-update-slice | bytes 16388 | tf_op jit(solution)/shard_map/scatter-add | solution.py:126
  485.3 4.7 scatter-add.71
  508.4 3.2 collective-permute-start.23
  516.1 9.1 %all-to-all-start.10 = ((f32[16,4,8,128]{3,2,1,0:T(8,128)}), f32[16,4,8,128]{3,2,1,0:T(8,128)S(1)}, u32[]{:S(2)}, u32[]{:S(2)}) async-start(f32[16,4,8,128]{3,2,1,0:T(8,128)} %stack.52), calls=%async_computation.10 | async-start | bytes 524288 | tf_op jit(solution)/shard_map/all_to_all | solution.py:72
  531.5 22.0 %scatter-add.75 = f32[4,8,64,128]{3,1,0,2:T(8,128)} dynamic-update-slice(f32[4,8,64,128]{3,1,0,2:T(8,128)} %slice.895, f32[4,8,64,1]{3,1,0,2:T(8,128)} %slice_add_fusion.5, s32[]{:T(128)} %constant.410.clone.1, s32[]{:T(128)} %constant.410.clone.1, s32[]{:T(128)} %constant.410.clone.1, s32[]{:T(128)} %constant.416.clone.1) | dynamic-update-slice | bytes 16388 | tf_op jit(solution)/shard_map/scatter-add | solution.py:126
  556.3 4.7 scatter-add.76
  579.3 3.2 collective-permute-start.25
  586.9 8.8 %all-to-all-start.11 = ((f32[16,4,8,128]{3,2,1,0:T(8,128)}), f32[16,4,8,128]{3,2,1,0:T(8,128)S(1)}, u32[]{:S(2)}, u32[]{:S(2)}) async-start(f32[16,4,8,128]{3,2,1,0:T(8,128)} %stack.54), calls=%async_computation.11 | async-start | bytes 524288 | tf_op jit(solution)/shard_map/all_to_all | solution.py:72
  602.4 22.0 %scatter-add.80 = f32[4,8,64,128]{3,1,0,2:T(8,128)} dynamic-update-slice(f32[4,8,64,128]{3,1,0,2:T(8,128)} %slice.901, f32[4,8,64,1]{3,1,0,2:T(8,128)} %slice_add_fusion.3, s32[]{:T(128)} %constant.410.clone.1, s32[]{:T(128)} %constant.410.clone.1, s32[]{:T(128)} %constant.410.clone.1, s32[]{:T(128)} %constant.416.clone.1) | dynamic-update-slice | bytes 16388 | tf_op jit(solution)/shard_map/scatter-add | solution.py:126
  627.1 4.7 scatter-add.81
  639.5 7.4 %multiply_reduce_fusion.4 = (f32[8,64,128]{2,0,1:T(8,128)S(1)}, f32[8,64,128]{2,0,1:T(8,128)S(1)}, f32[8,64,128]{2,0,1:T(8,128)}, f32[8,64,128]{2,0,1:T(8,128)},...) fusion(f32[4,8,64,128]{3,1,0,2:T(8,128)} %get-tuple-element.250, ...), kind=kLoop, calls=%fused_computation.135 | loop fusion | flops 5111808 | bytes 17301504 | tf_op jit(solution)/shard_map/transpose(jvp())/reduce_sum | solution.py:63
  653.1 3.1 collective-permute-start.27
  661.4 9.1 %all-to-all-start.12 = ((f32[16,4,8,128]{3,2,1,0:T(8,128)}), f32[16,4,8,128]{3,2,1,0:T(8,128)S(1)}, u32[]{:S(2)}, u32[]{:S(2)}) async-start(f32[16,4,8,128]{3,2,1,0:T(8,128)} %stack.56), calls=%async_computation.12 | async-start | bytes 524288 | tf_op jit(solution)/shard_map/all_to_all | solution.py:72
  676.0 20.7 %scatter-add.85 = f32[4,8,64,128]{3,1,0,2:T(8,128)S(1)} dynamic-update-slice(f32[4,8,64,128]{3,1,0,2:T(8,128)S(1)} %slice.907, f32[4,8,64,1]{3,1,0,2:T(8,128)S(1)} %slice_add_fusion.1, s32[]{:T(128)} %constant.410.clone.1, s32[]{:T(128)} %constant.410.clone.1, s32[]{:T(128)} %constant.410.clone.1, s32[]{:T(128)} %constant.416.clone.1) | dynamic-update-slice | bytes 16388 | tf_op jit(solution)/shard_map/scatter-add | solution.py:126
  698.1 3.5 scatter-add.86
  (347 shorter events, 319.6 us)
Async XLA Ops:
  8.8 32.8 %all-to-all-start = ((f32[16,1,8,128]{3,2,1,0:T(8,128)}), f32[16,1,8,128]{3,2,1,0:T(8,128)S(1)}, u32[]{:S(2)}, u32[]{:S(2)}) async-start(f32[16,1,8,128]{3,2,1,0:T(8,128)} %stack.38), calls=%async_computation | async-start | bytes 131072 | tf_op jit(solution)/shard_map/all_to_all | solution.py:72
  19.0 15.9 %collective-permute-start = (f32[1,8,64,1]{3,2,1,0:T(8,128)}, f32[1,8,64,1]{3,2,1,0:T(8,128)S(1)}, u32[]{:S(2)}, u32[]{:S(2)}) collective-permute-start(f32[1,8,64,1]{3,2,1,0:T(8,128)} %get-tuple-element.333), channel_id=1, source_target_pairs={{0,8},{8,16},{16,24},{24,32},{32,40},{40,48},{48,56},{56,64},{64,7... | collective-permute-start | bytes 6152 | tf_op jit(solution)/shard_map/ppermute | solution.py:16
  22.1 12.8 %collective-permute-start.1 = (f32[1,8,64,1]{3,2,1,0:T(8,128)S(1)}, f32[1,8,64,1]{3,2,1,0:T(8,128)S(1)}, u32[]{:S(2)}, u32[]{:S(2)}) collective-permute-start(f32[1,8,64,1]{3,2,1,0:T(8,128)S(1)} %get-tuple-element.334), channel_id=1, source_target_pairs={{8,0},{16,8},{24,16},{32,24},{40,32},{48,40},{56,48},{64,56},{72,6... | collective-permute-start | bytes 6152 | tf_op jit(solution)/shard_map/ppermute | solution.py:18
  27.4 12.4 %collective-permute-start.3 = (f32[4,8,64,1]{2,1,3,0:T(8,128)S(1)}, f32[4,8,64,1]{2,1,3,0:T(8,128)S(1)}, u32[]{:S(2)}, u32[]{:S(2)}) collective-permute-start(f32[4,8,64,1]{2,1,3,0:T(8,128)S(1)} %copy.1084), channel_id=1, source_target_pairs={{0,8},{8,16},{16,24},{24,32},{32,40},{40,48},{48,56},{56,64},{64,7... | collective-permute-start | bytes 24584 | tf_op jit(solution)/shard_map/ppermute | solution.py:16
  32.5 4.8 collective-permute-start.2
  42.4 16.5 %all-to-all-start.1 = ((f32[16,4,8,128]{3,2,1,0:T(8,128)}), f32[16,4,8,128]{3,2,1,0:T(8,128)S(1)}, u32[]{:S(2)}, u32[]{:S(2)}) async-start(f32[16,4,8,128]{3,2,1,0:T(8,128)} %stack.39), calls=%async_computation.1 | async-start | bytes 524288 | tf_op jit(solution)/shard_map/all_to_all | solution.py:72
  71.8 11.3 %copy-start.1 = (f32[4,8,64,128]{3,1,0,2:T(8,128)S(1)}, f32[4,8,64,128]{3,1,0,2:T(8,128)}, u32[]{:S(2)}) copy-start(f32[4,8,64,128]{3,1,0,2:T(8,128)} %copy-done) | copy-start | bytes 3145732
  71.8 19.7 %all-to-all-start.2 = ((f32[16,4,8,128]{3,2,1,0:T(8,128)}), f32[16,4,8,128]{3,2,1,0:T(8,128)S(1)}, u32[]{:S(2)}, u32[]{:S(2)}) async-start(f32[16,4,8,128]{3,2,1,0:T(8,128)} %stack.40), calls=%async_computation.2 | async-start | bytes 524288 | tf_op jit(solution)/shard_map/all_to_all | solution.py:72
  79.8 9.9 %collective-permute-start.5 = (f32[4,8,64,1]{2,1,3,0:T(8,128)S(1)}, f32[4,8,64,1]{2,1,3,0:T(8,128)S(1)}, u32[]{:S(2)}, u32[]{:S(2)}) collective-permute-start(f32[4,8,64,1]{2,1,3,0:T(8,128)S(1)} %copy.1095), channel_id=1, source_target_pairs={{0,8},{8,16},{16,24},{24,32},{32,40},{40,48},{48,56},{56,64},{64,7... | collective-permute-start | bytes 24584 | tf_op jit(solution)/shard_map/ppermute | solution.py:16
  82.9 4.9 collective-permute-start.4
  104.4 12.8 %copy-start.3 = (f32[4,8,64,128]{3,1,0,2:T(8,128)S(1)}, f32[4,8,64,128]{3,1,0,2:T(8,128)}, u32[]{:S(2)}) copy-start(f32[4,8,64,128]{3,1,0,2:T(8,128)} %copy-done.2) | copy-start | bytes 3145732
  104.4 21.1 %all-to-all-start.3 = ((f32[16,4,8,128]{3,2,1,0:T(8,128)}), f32[16,4,8,128]{3,2,1,0:T(8,128)S(1)}, u32[]{:S(2)}, u32[]{:S(2)}) async-start(f32[16,4,8,128]{3,2,1,0:T(8,128)} %stack.41), calls=%async_computation.3 | async-start | bytes 524288 | tf_op jit(solution)/shard_map/all_to_all | solution.py:72
  114.0 9.7 %collective-permute-start.7 = (f32[4,8,64,1]{2,1,3,0:T(8,128)S(1)}, f32[4,8,64,1]{2,1,3,0:T(8,128)S(1)}, u32[]{:S(2)}, u32[]{:S(2)}) collective-permute-start(f32[4,8,64,1]{2,1,3,0:T(8,128)S(1)} %copy.1102), channel_id=1, source_target_pairs={{0,8},{8,16},{16,24},{24,32},{32,40},{40,48},{48,56},{56,64},{64,7... | collective-permute-start | bytes 24584 | tf_op jit(solution)/shard_map/ppermute | solution.py:16
  117.2 4.7 collective-permute-start.6
  138.5 13.1 %copy-start.5 = (f32[4,8,64,128]{3,1,0,2:T(8,128)S(1)}, f32[4,8,64,128]{3,1,0,2:T(8,128)}, u32[]{:S(2)}) copy-start(f32[4,8,64,128]{3,1,0,2:T(8,128)} %copy-done.4) | copy-start | bytes 3145732
  138.5 21.4 %all-to-all-start.4 = ((f32[16,4,8,128]{3,2,1,0:T(8,128)}), f32[16,4,8,128]{3,2,1,0:T(8,128)S(1)}, u32[]{:S(2)}, u32[]{:S(2)}) async-start(f32[16,4,8,128]{3,2,1,0:T(8,128)} %stack.42), calls=%async_computation.4 | async-start | bytes 524288 | tf_op jit(solution)/shard_map/all_to_all | solution.py:72
  148.1 10.0 %collective-permute-start.9 = (f32[4,8,64,1]{2,1,3,0:T(8,128)S(1)}, f32[4,8,64,1]{2,1,3,0:T(8,128)S(1)}, u32[]{:S(2)}, u32[]{:S(2)}) collective-permute-start(f32[4,8,64,1]{2,1,3,0:T(8,128)S(1)} %copy.1109), channel_id=1, source_target_pairs={{0,8},{8,16},{16,24},{24,32},{32,40},{40,48},{48,56},{56,64},{64,7... | collective-permute-start | bytes 24584 | tf_op jit(solution)/shard_map/ppermute | solution.py:16
  151.2 5.1 collective-permute-start.8
  172.8 12.7 %copy-start.7 = (f32[4,8,64,128]{3,1,0,2:T(8,128)S(1)}, f32[4,8,64,128]{3,1,0,2:T(8,128)}, u32[]{:S(2)}) copy-start(f32[4,8,64,128]{3,1,0,2:T(8,128)} %copy-done.6) | copy-start | bytes 3145732
  172.8 21.0 %all-to-all-start.5 = ((f32[16,4,8,128]{3,2,1,0:T(8,128)}), f32[16,4,8,128]{3,2,1,0:T(8,128)S(1)}, u32[]{:S(2)}, u32[]{:S(2)}) async-start(f32[16,4,8,128]{3,2,1,0:T(8,128)} %stack.43), calls=%async_computation.5 | async-start | bytes 524288 | tf_op jit(solution)/shard_map/all_to_all | solution.py:72
  182.4 9.7 %collective-permute-start.11 = (f32[4,8,64,1]{2,1,3,0:T(8,128)S(1)}, f32[4,8,64,1]{2,1,3,0:T(8,128)S(1)}, u32[]{:S(2)}, u32[]{:S(2)}) collective-permute-start(f32[4,8,64,1]{2,1,3,0:T(8,128)S(1)} %copy.1116), channel_id=1, source_target_pairs={{0,8},{8,16},{16,24},{24,32},{32,40},{40,48},{48,56},{56,64},{64,7... | collective-permute-start | bytes 24584 | tf_op jit(solution)/shard_map/ppermute | solution.py:16
  185.6 4.7 collective-permute-start.10
  206.8 12.9 %copy-start.9 = (f32[4,8,64,128]{3,1,0,2:T(8,128)S(1)}, f32[4,8,64,128]{3,1,0,2:T(8,128)}, u32[]{:S(2)}) copy-start(f32[4,8,64,128]{3,1,0,2:T(8,128)} %copy-done.8) | copy-start | bytes 3145732
  206.8 21.2 %all-to-all-start.6 = ((f32[16,4,8,128]{3,2,1,0:T(8,128)}), f32[16,4,8,128]{3,2,1,0:T(8,128)S(1)}, u32[]{:S(2)}, u32[]{:S(2)}) async-start(f32[16,4,8,128]{3,2,1,0:T(8,128)} %stack.44), calls=%async_computation.6 | async-start | bytes 524288 | tf_op jit(solution)/shard_map/all_to_all | solution.py:72
  216.3 9.8 %collective-permute-start.13 = (f32[4,8,64,1]{2,1,3,0:T(8,128)S(1)}, f32[4,8,64,1]{2,1,3,0:T(8,128)S(1)}, u32[]{:S(2)}, u32[]{:S(2)}) collective-permute-start(f32[4,8,64,1]{2,1,3,0:T(8,128)S(1)} %copy.1123), channel_id=1, source_target_pairs={{0,8},{8,16},{16,24},{24,32},{32,40},{40,48},{48,56},{56,64},{64,7... | collective-permute-start | bytes 24584 | tf_op jit(solution)/shard_map/ppermute | solution.py:16
  219.5 4.8 collective-permute-start.12
  238.9 25.2 %collective-permute-start.14 = (f32[4,8,64,128]{3,1,0,2:T(8,128)}, f32[4,8,64,128]{3,1,0,2:T(8,128)S(1)}, u32[]{:S(2)}, u32[]{:S(2)}) collective-permute-start(f32[4,8,64,128]{3,1,0,2:T(8,128)} %get-tuple-element.247), channel_id=1, source_target_pairs={{0,1},{1,2},{2,3},{3,4},{4,5},{5,6},{6,7},{8,9},{9,10},{10,11},{11... | collective-permute-start | bytes 3145736 | tf_op jit(solution)/shard_map/ppermute | solution.py:28
  241.1 52.3 %copy-start.31 = (f32[1,4,8,64,128]{4,3,2,1,0:T(8,128)S(1)}, f32[1,4,8,64,128]{4,3,2,1,0:T(8,128)}, u32[]{:S(2)}) copy-start(f32[1,4,8,64,128]{4,3,2,1,0:T(8,128)} %param.45) | copy-start | bytes 3145732
  266.0 27.5 %collective-permute-start.15 = (f32[4,8,64,128]{3,1,0,2:T(8,128)S(1)}, f32[4,8,64,128]{3,1,0,2:T(8,128)S(1)}, u32[]{:S(2)}, u32[]{:S(2)}) collective-permute-start(f32[4,8,64,128]{3,1,0,2:T(8,128)S(1)} %subtract_select_fusion), channel_id=1, source_target_pairs={{1,0},{2,1},{3,2},{4,3},{5,4},{6,5},{7,6},{9,8},{10,9},{11,10},{12... | collective-permute-start | bytes 3145736 | tf_op jit(solution)/shard_map/ppermute | solution.py:28
  303.9 14.9 %collective-permute-start.16 = (f32[4,8,64]{2,1,0:T(8,128)S(1)}, f32[4,8,64]{2,1,0:T(8,128)S(1)}, u32[]{:S(2)}, u32[]{:S(2)}) collective-permute-start(f32[4,8,64]{2,1,0:T(8,128)S(1)} %bitcast.181), channel_id=1, source_target_pairs={{0,120},{8,0},{16,8},{24,16},{32,24},{40,32},{48,40},{56,48},{64,5... | collective-permute-start | bytes 24584 | tf_op jit(solution)/shard_map/ppermute | solution.py:34
  304.6 12.4 %collective-permute-start.17 = (f32[4,8,64]{2,1,0:T(8,128)S(1)}, f32[4,8,64]{2,1,0:T(8,128)S(1)}, u32[]{:S(2)}, u32[]{:S(2)}) collective-permute-start(f32[4,8,64]{2,1,0:T(8,128)S(1)} %bitcast.190), channel_id=1, source_target_pairs={{0,8},{8,16},{16,24},{24,32},{32,40},{40,48},{48,56},{56,64},{64,7... | collective-permute-start | bytes 24584 | tf_op jit(solution)/shard_map/ppermute | solution.py:34
  309.8 41.4 %all-to-all-start.7 = ((f32[16,4,8,128]{3,2,1,0:T(8,128)}), f32[16,4,8,128]{3,2,1,0:T(8,128)S(1)}, u32[]{:S(2)}, u32[]{:S(2)}) async-start(f32[16,4,8,128]{3,2,1,0:T(8,128)} %stack.46), calls=%async_computation.7 | async-start | bytes 524288 | tf_op jit(solution)/shard_map/all_to_all | solution.py:72
  366.5 18.7 %collective-permute-start.18 = (f32[4,8,64]{2,1,0:T(8,128)S(1)}, f32[4,8,64]{2,1,0:T(8,128)S(1)}, u32[]{:S(2)}, u32[]{:S(2)}) collective-permute-start(f32[4,8,64]{2,1,0:T(8,128)S(1)} %bitcast.183), channel_id=1, source_target_pairs={{0,120},{8,0},{16,8},{24,16},{32,24},{40,32},{48,40},{56,48},{64,5... | collective-permute-start | bytes 24584 | tf_op jit(solution)/shard_map/ppermute | solution.py:34
  366.5 16.9 %collective-permute-start.19 = (f32[4,8,64]{2,1,0:T(8,128)S(1)}, f32[4,8,64]{2,1,0:T(8,128)S(1)}, u32[]{:S(2)}, u32[]{:S(2)}) collective-permute-start(f32[4,8,64]{2,1,0:T(8,128)S(1)} %bitcast.191), channel_id=1, source_target_pairs={{0,8},{8,16},{16,24},{24,32},{32,40},{40,48},{48,56},{56,64},{64,7... | collective-permute-start | bytes 24584 | tf_op jit(solution)/shard_map/ppermute | solution.py:34
  374.1 45.1 %all-to-all-start.8 = ((f32[16,4,8,128]{3,2,1,0:T(8,128)}), f32[16,4,8,128]{3,2,1,0:T(8,128)S(1)}, u32[]{:S(2)}, u32[]{:S(2)}) async-start(f32[16,4,8,128]{3,2,1,0:T(8,128)} %stack.48), calls=%async_computation.8 | async-start | bytes 524288 | tf_op jit(solution)/shard_map/all_to_all | solution.py:72
  437.5 18.5 %collective-permute-start.20 = (f32[4,8,64]{2,1,0:T(8,128)S(1)}, f32[4,8,64]{2,1,0:T(8,128)S(1)}, u32[]{:S(2)}, u32[]{:S(2)}) collective-permute-start(f32[4,8,64]{2,1,0:T(8,128)S(1)} %bitcast.185), channel_id=1, source_target_pairs={{0,120},{8,0},{16,8},{24,16},{32,24},{40,32},{48,40},{56,48},{64,5... | collective-permute-start | bytes 24584 | tf_op jit(solution)/shard_map/ppermute | solution.py:34
  437.5 16.6 %collective-permute-start.21 = (f32[4,8,64]{2,1,0:T(8,128)S(1)}, f32[4,8,64]{2,1,0:T(8,128)S(1)}, u32[]{:S(2)}, u32[]{:S(2)}) collective-permute-start(f32[4,8,64]{2,1,0:T(8,128)S(1)} %bitcast.192), channel_id=1, source_target_pairs={{0,8},{8,16},{16,24},{24,32},{32,40},{40,48},{48,56},{56,64},{64,7... | collective-permute-start | bytes 24584 | tf_op jit(solution)/shard_map/ppermute | solution.py:34
  445.1 44.9 %all-to-all-start.9 = ((f32[16,4,8,128]{3,2,1,0:T(8,128)}), f32[16,4,8,128]{3,2,1,0:T(8,128)S(1)}, u32[]{:S(2)}, u32[]{:S(2)}) async-start(f32[16,4,8,128]{3,2,1,0:T(8,128)} %stack.50), calls=%async_computation.9 | async-start | bytes 524288 | tf_op jit(solution)/shard_map/all_to_all | solution.py:72
  508.4 18.6 %collective-permute-start.22 = (f32[4,8,64]{2,1,0:T(8,128)S(1)}, f32[4,8,64]{2,1,0:T(8,128)S(1)}, u32[]{:S(2)}, u32[]{:S(2)}) collective-permute-start(f32[4,8,64]{2,1,0:T(8,128)S(1)} %bitcast.187), channel_id=1, source_target_pairs={{0,120},{8,0},{16,8},{24,16},{32,24},{40,32},{48,40},{56,48},{64,5... | collective-permute-start | bytes 24584 | tf_op jit(solution)/shard_map/ppermute | solution.py:34
  508.4 16.7 %collective-permute-start.23 = (f32[4,8,64]{2,1,0:T(8,128)S(1)}, f32[4,8,64]{2,1,0:T(8,128)S(1)}, u32[]{:S(2)}, u32[]{:S(2)}) collective-permute-start(f32[4,8,64]{2,1,0:T(8,128)S(1)} %bitcast.193), channel_id=1, source_target_pairs={{0,8},{8,16},{16,24},{24,32},{32,40},{40,48},{48,56},{56,64},{64,7... | collective-permute-start | bytes 24584 | tf_op jit(solution)/shard_map/ppermute | solution.py:34
  516.1 44.9 %all-to-all-start.10 = ((f32[16,4,8,128]{3,2,1,0:T(8,128)}), f32[16,4,8,128]{3,2,1,0:T(8,128)S(1)}, u32[]{:S(2)}, u32[]{:S(2)}) async-start(f32[16,4,8,128]{3,2,1,0:T(8,128)} %stack.52), calls=%async_computation.10 | async-start | bytes 524288 | tf_op jit(solution)/shard_map/all_to_all | solution.py:72
  579.3 18.5 %collective-permute-start.24 = (f32[4,8,64]{2,1,0:T(8,128)S(1)}, f32[4,8,64]{2,1,0:T(8,128)S(1)}, u32[]{:S(2)}, u32[]{:S(2)}) collective-permute-start(f32[4,8,64]{2,1,0:T(8,128)S(1)} %bitcast.179), channel_id=1, source_target_pairs={{0,120},{8,0},{16,8},{24,16},{32,24},{40,32},{48,40},{56,48},{64,5... | collective-permute-start | bytes 24584 | tf_op jit(solution)/shard_map/ppermute | solution.py:34
  579.3 16.7 %collective-permute-start.25 = (f32[4,8,64]{2,1,0:T(8,128)S(1)}, f32[4,8,64]{2,1,0:T(8,128)S(1)}, u32[]{:S(2)}, u32[]{:S(2)}) collective-permute-start(f32[4,8,64]{2,1,0:T(8,128)S(1)} %bitcast.189), channel_id=1, source_target_pairs={{0,8},{8,16},{16,24},{24,32},{32,40},{40,48},{48,56},{56,64},{64,7... | collective-permute-start | bytes 24584 | tf_op jit(solution)/shard_map/ppermute | solution.py:34
  586.9 44.9 %all-to-all-start.11 = ((f32[16,4,8,128]{3,2,1,0:T(8,128)}), f32[16,4,8,128]{3,2,1,0:T(8,128)S(1)}, u32[]{:S(2)}, u32[]{:S(2)}) async-start(f32[16,4,8,128]{3,2,1,0:T(8,128)} %stack.54), calls=%async_computation.11 | async-start | bytes 524288 | tf_op jit(solution)/shard_map/all_to_all | solution.py:72
  595.7 114.0 %reduce-scatter.2.cloned.1.call-start = ((), (), s32[]{:S(2)}) async-start(), calls=%async_computation.14 | async-start | bytes 294912 | tf_op jit(solution)/shard_map/reduce_scatter | solution.py:130
  653.0 19.4 %collective-permute-start.26 = (f32[4,8,64]{2,1,0:T(8,128)S(1)}, f32[4,8,64]{2,1,0:T(8,128)S(1)}, u32[]{:S(2)}, u32[]{:S(2)}) collective-permute-start(f32[4,8,64]{2,1,0:T(8,128)S(1)} %bitcast.175), channel_id=1, source_target_pairs={{0,120},{8,0},{16,8},{24,16},{32,24},{40,32},{48,40},{56,48},{64,5... | collective-permute-start | bytes 24584 | tf_op jit(solution)/shard_map/ppermute | solution.py:34
  653.1 17.5 %collective-permute-start.27 = (f32[4,8,64]{2,1,0:T(8,128)S(1)}, f32[4,8,64]{2,1,0:T(8,128)S(1)}, u32[]{:S(2)}, u32[]{:S(2)}) collective-permute-start(f32[4,8,64]{2,1,0:T(8,128)S(1)} %bitcast.177), channel_id=1, source_target_pairs={{0,8},{8,16},{16,24},{24,32},{32,40},{40,48},{48,56},{56,64},{64,7... | collective-permute-start | bytes 24584 | tf_op jit(solution)/shard_map/ppermute | solution.py:34
  661.4 40.2 %all-to-all-start.12 = ((f32[16,4,8,128]{3,2,1,0:T(8,128)}), f32[16,4,8,128]{3,2,1,0:T(8,128)S(1)}, u32[]{:S(2)}, u32[]{:S(2)}) async-start(f32[16,4,8,128]{3,2,1,0:T(8,128)} %stack.56), calls=%async_computation.12 | async-start | bytes 524288 | tf_op jit(solution)/shard_map/all_to_all | solution.py:72
  (29 other events, 64.4 us)
Sparse Core Ops, SparseCore 0:
  660.8 37.7 reduce-scatter.1
